TPU v7x, 32 devices: a whole 2x2x4 slice. The times are simulated.
32 devices in a mesh: replica: 8 (over y, x, core), fsdp: 4 (over z).
Axes of the slice: x: 2, y: 2, z: 4, core: 2. Of those that a mesh axis runs over, the one named last changes fastest.
Arguments:
- momentum: bfloat16 [8, 4, 384, 1024], P('replica', None, 'fsdp'), may hold values from -400 to 400
- weights: bfloat16 [8, 4, 384, 1024], P('replica', 'fsdp'), may hold values from -6 to 6
- tokens: bfloat16 [8, 1024, 1024], P('replica', 'fsdp'), may hold values from -6 to 6
- routes: int32 [8, 1024, 1], P('replica', 'fsdp'), may hold values from 0 to 3; in each aligned block of 256 rows (0 to 255, 256 to 511, ..., all dimensions but the last counted through in order) at most 128 rows name the same one
Outputs:
- new_weight: bfloat16 [8, 4, 384, 1024], P('replica', 'fsdp')
- expert_rows: bfloat16 [8, 4, 512, 384], P('replica', 'fsdp')
Inputs may be any that keep to these rules, and one draw needn't show every extreme that they name: `routes`: within one replica, the 256 rows of one device name each expert at most 128 times, a bound that some block reaches.
All inputs are finite; a program needn't handle non-finite values.
Results may differ from a plain program's by a relative error of at most 0.008.
Values may be sent and summed in bfloat16 or wider, within the bound.
No kernel may reach another device: no remote copies, remote signals or barrier semaphores. Data moves between devices by JAX's collectives and lax.ppermute only.
A program may use at most 64 MiB of HBM per device.

v0:
```python
import math
import jax
import jax.numpy as jnp
from jax import lax
from jax.sharding import PartitionSpec as P

ITERS = 2
GOSSIP_BIT = 2
coef_a = 3.4445
coef_b = -4.775
coef_c = 2.0315
step_rate = 0.5


def from_partner(shard, axis, bit):
    return lax.ppermute(shard, axis, [(i, i ^ 1 << bit) for i in range(lax.axis_size(axis))])


def orthogonalize(matrix):
    values = matrix.astype(jnp.float32)
    ortho = (values / (jnp.sqrt(jnp.sum(values * values)) + 1e-07)).astype(jnp.bfloat16)
    for step in range(ITERS):
        gram = jnp.einsum("fd,gd->fg", ortho, ortho, preferred_element_type=jnp.float32).astype(
            jnp.bfloat16
        )
        poly = (
            coef_b * gram.astype(jnp.float32)
            + coef_c * jnp.dot(gram, gram, preferred_element_type=jnp.float32)
        ).astype(jnp.bfloat16)
        ortho = (
            coef_a * ortho.astype(jnp.float32)
            + jnp.dot(poly, ortho, preferred_element_type=jnp.float32)
        ).astype(jnp.bfloat16)
    return ortho


def apply_update(weight, ortho, width):
    return (
        weight.astype(jnp.float32) - step_rate * math.sqrt(width) * ortho.astype(jnp.float32)
    ).astype(jnp.bfloat16)


def per_device(momentum, weights, tokens, routes):
    nodes = lax.axis_size("fsdp")
    experts = momentum.shape[1]
    width = momentum.shape[3]
    tok_rows = tokens.shape[1]
    capacity = 2 * tok_rows // nodes
    expert_id = routes[0, :, 0]
    onehot = (expert_id[:, None] == jnp.arange(experts, dtype=jnp.int32)[None, :]).astype(jnp.int32)
    position = jnp.sum((jnp.cumsum(onehot, axis=0) - 1) * onehot, axis=1)
    slot_id = expert_id * capacity + position
    placing = (slot_id[None, :] == jnp.arange(experts * capacity, dtype=jnp.int32)[:, None]).astype(
        jnp.bfloat16
    )
    packed = jnp.dot(placing, tokens[0], preferred_element_type=jnp.float32).astype(jnp.bfloat16)
    packed = packed.reshape(experts, capacity, width)
    arrived = lax.all_to_all(packed, "fsdp", split_axis=0, concat_axis=1, tiled=True)
    gathered = lax.all_to_all(momentum[0], "fsdp", split_axis=0, concat_axis=1, tiled=True)
    matrix = gathered[0]
    own_weight = weights[0, 0]
    updated = apply_update(own_weight, orthogonalize(matrix), width)
    partner = from_partner(updated, "replica", GOSSIP_BIT)
    averaged = (0.5 * (updated.astype(jnp.float32) + partner.astype(jnp.float32))).astype(
        jnp.bfloat16
    )
    projected = jnp.einsum("sd,fd->sf", arrived[0], averaged, preferred_element_type=jnp.float32)
    expert_rows = (projected / math.sqrt(width)).astype(jnp.bfloat16)
    return (averaged[None, None], expert_rows[None, None])


def solution(mesh):
    in_specs = (
        P("replica", None, "fsdp", None),
        P("replica", "fsdp", None, None),
        P("replica", "fsdp", None),
        P("replica", "fsdp", None),
    )
    out_specs = (P("replica", "fsdp", None, None), P("replica", "fsdp", None, None))
    return jax.shard_map(
        per_device, mesh=mesh, in_specs=in_specs, out_specs=out_specs, check_vma=False
    )
```

profile of v0, /device:TPU:0, one launch (start us, length us, event | category | flops | bytes accessed | tf_op | source)
XLA Modules:
  0.0 59.8 jit_solution(4275068450957944192)
XLA Ops:
  0.6 0.0 copy-start
  0.7 6.5 %all-to-all-start = ((bf16[4,96,1024]{2,1,0:T(8,128)(2,1)}), bf16[4,96,1024]{2,1,0:T(8,128)(2,1)S(1)}, u32[]{:S(2)}, u32[]{:S(2)}) async-start(bf16[4,96,1024]{2,1,0:T(8,128)(2,1)} %bitcast.43), calls=%async_computation | async-start | bytes 1572864 | tf_op jit(solution)/shard_map/all_to_all | solution.py:59
  7.2 1.2 %reduce-window.6 = s32[4,2,128]{2,1,0:T(2,128)S(1)} reduce-window(s32[4,2,128]{2,1,0:T(2,128)S(1)} %compare_convert_fusion, s32[]{:T(128)} %constant.25.clone.1), window={size=1x1x128 pad=0_0x0_0x127_0}, to_apply=%region_1.2 | reduce-window | flops 130048 | bytes 8196 | tf_op jit(solution)/shard_map/reduce-window
  8.4 0.1 slice.8
  8.5 0.1 copy.6
  8.6 0.1 copy.7
  8.7 0.1 add_bitcast_fusion
  8.8 1.4 %convolution_convert_fusion = bf16[512,1024]{1,0:T(8,128)(2,1)} fusion(bf16[1,256,1024]{2,1,0:T(8,128)(2,1)S(1)} %copy-done, s32[256]{0:T(256)S(1)} %multiply_add_fusion), kind=kOutput, calls=%fused_computation.9 | convolution fusion | flops 269090816 | bytes 1573888 | tf_op jit(solution)/shard_map/dot_general | solution.py:56
  10.3 17.0 %all-to-all-done = bf16[4,96,1024]{2,1,0:T(8,128)(2,1)S(1)} async-done(((bf16[4,96,1024]{2,1,0:T(8,128)(2,1)}), bf16[4,96,1024]{2,1,0:T(8,128)(2,1)S(1)}, u32[]{:S(2)}, u32[]{:S(2)}) %all-to-all-start) | async-done | bytes 786464 | tf_op jit(solution)/shard_map/all_to_all | solution.py:59
  27.3 3.5 %all-to-all-start.1 = ((bf16[4,128,1024]{2,1,0:T(8,128)(2,1)}), bf16[4,128,1024]{2,1,0:T(8,128)(2,1)S(1)}, u32[]{:S(2)}, u32[]{:S(2)}) async-start(bf16[4,128,1024]{2,1,0:T(8,128)(2,1)} %bitcast.9), calls=%async_computation.1 | async-start | bytes 2097152 | tf_op jit(solution)/shard_map/all_to_all | solution.py:58
  30.8 1.0 %fusion = f32[]{:T(128)} fusion(bf16[4,96,1024]{2,1,0:T(8,128)(2,1)S(1)} %all-to-all-done), kind=kLoop, calls=%fused_computation.2 | loop fusion | flops 1179647 | bytes 786436 | tf_op jit(solution)/shard_map/reduce_sum | solution.py:21
  32.5 0.2 fusion.1
  32.7 0.6 convolution_convert_fusion.2
  33.3 0.8 %add_convert_fusion.1 = bf16[384,1024]{1,0:T(8,128)(2,1)S(1)} fusion(bf16[384,1024]{1,0:T(8,128)(2,1)S(1)} %bitcast.45, bf16[384,384]{1,0:T(8,128)(2,1)S(1)} %convolution_convert_fusion.2), kind=kOutput, calls=%fused_computation.8 | convolution fusion | flops 417546240 | bytes 1867776 | tf_op jit(solution)/shard_map/dot_general | solution.py:32
  34.1 0.0 copy-start.3
  34.1 0.9 %copy-done.3 = bf16[384,1024]{1,0:T(8,128)(2,1)} copy-done((bf16[384,1024]{1,0:T(8,128)(2,1)}, bf16[384,1024]{1,0:T(8,128)(2,1)S(1)}, u32[]{:S(2)}) %copy-start.3) | copy-done | bytes 786456
  35.0 0.6 convolution_convert_fusion.1
  35.6 0.5 copy-done.2
  36.1 2.4 %fusion.2 = bf16[384,1024]{1,0:T(8,128)(2,1)S(1)} fusion(bf16[384,1024]{1,0:T(8,128)(2,1)} %copy-done.3, bf16[384,384]{1,0:T(8,128)(2,1)S(1)} %convolution_convert_fusion.1, bf16[1,1,384,1024]{3,2,1,0:T(8,128)(2,1)S(1)} %copy-done.2), kind=kOutput, calls=%fused_computation.5 | convolution fusion | flops 419512320 | bytes 2654208 | tf_op jit(solution)/shard_map/dot_general | solution.py:32
  38.5 1.6 %collective-permute-start = (bf16[384,1024]{1,0:T(8,128)(2,1)S(1)}, bf16[384,1024]{1,0:T(8,128)(2,1)S(1)}, u32[]{:S(2)}, u32[]{:S(2)}) collective-permute-start(bf16[384,1024]{1,0:T(8,128)(2,1)S(1)} %fusion.2), channel_id=1, source_target_pairs={{0,16},{4,20},{8,24},{12,28},{16,0},{20,4},{24,8},{28,12},{1,17},{... | collective-permute-start | bytes 2359304 | tf_op jit(solution)/shard_map/ppermute | solution.py:16
  40.1 17.0 %collective-permute-done = bf16[384,1024]{1,0:T(8,128)(2,1)S(1)} collective-permute-done((bf16[384,1024]{1,0:T(8,128)(2,1)S(1)}, bf16[384,1024]{1,0:T(8,128)(2,1)S(1)}, u32[]{:S(2)}, u32[]{:S(2)}) %collective-permute-start) | collective-permute-done | bytes 786464 | tf_op jit(solution)/shard_map/ppermute | solution.py:16
  57.1 1.2 %fusion.19 = bf16[1,1,384,1024]{3,2,1,0:T(8,128)(2,1)} fusion(bf16[384,1024]{1,0:T(8,128)(2,1)S(1)} %collective-permute-done, bf16[384,1024]{1,0:T(8,128)(2,1)S(1)} %fusion.2), kind=kLoop, calls=%fused_computation.32 | loop fusion | flops 1966080 | bytes 2359296 | tf_op jit(solution)/shard_map/broadcast_in_dim | solution.py:69
  58.3 0.0 all-to-all-done.1
  58.3 1.5 %fusion.8 = bf16[1,1,512,384]{3,2,1,0:T(8,128)(2,1)} fusion(bf16[512,1024]{1,0:T(8,128)(2,1)S(1)} %bitcast.42, bf16[384,1024]{1,0:T(8,128)(2,1)S(1)} %collective-permute-done, bf16[384,1024]{1,0:T(8,128)(2,1)S(1)} %fusion.2), kind=kOutput, calls=%fused_computation.20 | convolution fusion | flops 405012480 | bytes 3014656 | tf_op jit(solution)/shard_map/sd,fd->sf/dot_general | solution.py:67
  (9 shorter events, 0.1 us)
Async XLA Ops:
  0.6 8.2 %copy-start = (bf16[1,256,1024]{2,1,0:T(8,128)(2,1)S(1)}, bf16[1,256,1024]{2,1,0:T(8,128)(2,1)}, u32[]{:S(2)}) copy-start(bf16[1,256,1024]{2,1,0:T(8,128)(2,1)} %param.6) | copy-start | bytes 1572868
  0.6 6.5 %copy-start.1 = (s32[1,256,1]{1,2,0:T(1,128)S(1)}, s32[1,256,1]{1,2,0:T(1,128)}, u32[]{:S(2)}) copy-start(s32[1,256,1]{1,2,0:T(1,128)} %param.7) | copy-start | bytes 3076
  0.7 26.6 %all-to-all-start = ((bf16[4,96,1024]{2,1,0:T(8,128)(2,1)}), bf16[4,96,1024]{2,1,0:T(8,128)(2,1)S(1)}, u32[]{:S(2)}, u32[]{:S(2)}) async-start(bf16[4,96,1024]{2,1,0:T(8,128)(2,1)} %bitcast.43), calls=%async_computation | async-start | bytes 1572864 | tf_op jit(solution)/shard_map/all_to_all | solution.py:59
  27.3 31.1 %all-to-all-start.1 = ((bf16[4,128,1024]{2,1,0:T(8,128)(2,1)}), bf16[4,128,1024]{2,1,0:T(8,128)(2,1)S(1)}, u32[]{:S(2)}, u32[]{:S(2)}) async-start(bf16[4,128,1024]{2,1,0:T(8,128)(2,1)} %bitcast.9), calls=%async_computation.1 | async-start | bytes 2097152 | tf_op jit(solution)/shard_map/all_to_all | solution.py:58
  34.1 0.9 %copy-start.3 = (bf16[384,1024]{1,0:T(8,128)(2,1)}, bf16[384,1024]{1,0:T(8,128)(2,1)S(1)}, u32[]{:S(2)}) copy-start(bf16[384,1024]{1,0:T(8,128)(2,1)S(1)} %add_convert_fusion.1) | copy-start | bytes 2359300
  35.0 1.1 %copy-start.2 = (bf16[1,1,384,1024]{3,2,1,0:T(8,128)(2,1)S(1)}, bf16[1,1,384,1024]{3,2,1,0:T(8,128)(2,1)}, u32[]{:S(2)}) copy-start(bf16[1,1,384,1024]{3,2,1,0:T(8,128)(2,1)} %param.5) | copy-start | bytes 2359300
  38.5 18.6 %collective-permute-start = (bf16[384,1024]{1,0:T(8,128)(2,1)S(1)}, bf16[384,1024]{1,0:T(8,128)(2,1)S(1)}, u32[]{:S(2)}, u32[]{:S(2)}) collective-permute-start(bf16[384,1024]{1,0:T(8,128)(2,1)S(1)} %fusion.2), channel_id=1, source_target_pairs={{0,16},{4,20},{8,24},{12,28},{16,0},{20,4},{24,8},{28,12},{1,17},{... | collective-permute-start | bytes 2359304 | tf_op jit(solution)/shard_map/ppermute | solution.py:16
where the time goes:
time: 60.2 us; the launch traced here: 59.8 us
  waiting for transfers between devices  34 us (56%)
  starting transfers between devices  11.6 us (19%)
  matrix products  7.35 us (12%)
  other arithmetic  3.72 us (6%)
  local copies, waits for them, and re-layouts  1.7 us (3%)
  between operations  1.41 us (2%)
    ppermute x1, waiting for transfers between devices, from_partner(): lax.ppermute(shard, axis, [(i, i ^ 1 << bit) for i in range(lax.axis_size...  17 us
    all_to_all x1, waiting for transfers between devices, per_device(): lax.all_to_all(momentum[0], 'fsdp', split_axis=0, concat_axis=1, tiled=True)  17 us
    all_to_all x1, starting transfers between devices, per_device(): lax.all_to_all(momentum[0], 'fsdp', split_axis=0, concat_axis=1, tiled=True)  6.49 us
    all_to_all x1, starting transfers between devices, per_device(): lax.all_to_all(packed, 'fsdp', split_axis=0, concat_axis=1, tiled=True)  3.52 us
    dot_general x2, matrix products, orthogonalize(): jnp.dot(poly, ortho, preferred_element_type=jnp.float32)  3.23 us
    ppermute x1, starting transfers between devices, from_partner(): lax.ppermute(shard, axis, [(i, i ^ 1 << bit) for i in range(lax.axis_size...  1.59 us
    dot_general x1, matrix products, per_device(): jnp.einsum('sd,fd->sf', arrived[0], averaged, preferred_element_type=jnp....  1.5 us
    dot_general x1, matrix products, per_device(): jnp.dot(placing, tokens[0], preferred_element_type=jnp.float32)  1.44 us
  transfers between devices with their start and end apart: 3, of which 2 were waited for; matrix products, arithmetic and copies ran while one was open for 16% of the time, Pallas kernels for 0%

commit v1 on v0

--- a/solution.py
+++ b/solution.py
@@ -55,7 +55,10 @@
     )
     packed = jnp.dot(placing, tokens[0], preferred_element_type=jnp.float32).astype(jnp.bfloat16)
     packed = packed.reshape(experts, capacity, width)
-    arrived = lax.all_to_all(packed, "fsdp", split_axis=0, concat_axis=1, tiled=True)
+    arrived = jnp.concatenate(
+        lax.all_to_all(jnp.stack(jnp.split(packed, lax.axis_size("fsdp"), axis=0)), "fsdp", 0, 0),
+        axis=1,
+    )
     gathered = lax.all_to_all(momentum[0], "fsdp", split_axis=0, concat_axis=1, tiled=True)
     matrix = gathered[0]
     own_weight = weights[0, 0]

time: 60.2 us -> 60.2 us (level)
  other arithmetic: 3.72 us -> 4.85 us
  matrix products: 7.35 us -> 6.36 us
    another operation x2 -> x3, other arithmetic: 1.26 us -> 2.39 us
    dot_general x1, matrix products: 1.44 us -> 0.44 us  [per_device(): jnp.dot(placing, tokens[0], preferred_element_type=jnp.float32)]
  transfers between devices with their start and end apart: 3 -> 3, of which waited for: 2 -> 2; matrix products, arithmetic and copies ran while one was open for 16% -> 17% of each run, Pallas kernels for 0% -> 0%
where the time goes in v1:
time: 60.2 us; the launch traced here: 59.8 us
  waiting for transfers between devices  33.8 us (56%)
  starting transfers between devices  11.6 us (19%)
  matrix products  6.36 us (11%)
  other arithmetic  4.85 us (8%)
  local copies, waits for them, and re-layouts  1.77 us (3%)
  between operations  1.42 us (2%)
    ppermute x1, waiting for transfers between devices, from_partner(): lax.ppermute(shard, axis, [(i, i ^ 1 << bit) for i in range(lax.axis_size...  17 us
    all_to_all x1, waiting for transfers between devices, per_device(): lax.all_to_all(momentum[0], 'fsdp', split_axis=0, concat_axis=1, tiled=True)  16.8 us
    all_to_all x1, starting transfers between devices, per_device(): lax.all_to_all(momentum[0], 'fsdp', split_axis=0, concat_axis=1, tiled=True)  6.49 us
    all_to_all x1, starting transfers between devices, per_device(): lax.all_to_all(jnp.stack(jnp.split(packed, lax.axis_size('fsdp'), axis=0)...  3.52 us
    dot_general x2, matrix products, orthogonalize(): jnp.dot(poly, ortho, preferred_element_type=jnp.float32)  3.24 us
    ppermute x1, starting transfers between devices, from_partner(): lax.ppermute(shard, axis, [(i, i ^ 1 << bit) for i in range(lax.axis_size...  1.58 us
    dot_general x1, matrix products, per_device(): jnp.einsum('sd,fd->sf', arrived[0], averaged, preferred_element_type=jnp....  1.5 us
    unnamed x8, local copies, waits for them, and re-layouts  1.43 us
  transfers between devices with their start and end apart: 3, of which 2 were waited for; matrix products, arithmetic and copies ran while one was open for 17% of the time, Pallas kernels for 0%

profile of v1, /device:TPU:0, one launch (start us, length us, event | category | flops | bytes accessed | tf_op | source)
XLA Modules:
  0.0 59.8 jit_solution(14235260171432248929)
XLA Ops:
  0.6 0.0 copy-start
  0.7 6.5 %all-to-all-start = ((bf16[4,96,1024]{2,1,0:T(8,128)(2,1)}), bf16[4,96,1024]{2,1,0:T(8,128)(2,1)S(1)}, u32[]{:S(2)}, u32[]{:S(2)}) async-start(bf16[4,96,1024]{2,1,0:T(8,128)(2,1)} %bitcast.50), calls=%async_computation | async-start | bytes 1572864 | tf_op jit(solution)/shard_map/all_to_all | solution.py:62
  7.2 1.2 %reduce-window.6 = s32[4,2,128]{2,1,0:T(2,128)S(1)} reduce-window(s32[4,2,128]{2,1,0:T(2,128)S(1)} %compare_convert_fusion, s32[]{:T(128)} %constant.25.clone.1), window={size=1x1x128 pad=0_0x0_0x127_0}, to_apply=%region_1.2 | reduce-window | flops 130048 | bytes 8196 | tf_op jit(solution)/shard_map/reduce-window
  8.4 0.1 slice.12
  8.5 0.1 copy.6
  8.6 0.1 copy.7
  8.7 0.1 add_bitcast_fusion
  8.8 0.4 convolution_convert_fusion
  9.3 0.1 slice_bitcast_fusion.3
  9.3 1.1 %pad_maximum_fusion = bf16[4,1,128,1024]{3,2,1,0:T(8,128)(2,1)} fusion(bf16[1,1,128,1024]{3,2,1,0:T(8,128)(2,1)S(1)} %get-tuple-element.3, bf16[1,1,128,1024]{3,2,1,0:T(8,128)(2,1)S(1)} %get-tuple-element.4, bf16[1,1,128,1024]{3,2,1,0:T(8,128)(2,1)S(1)} %get-tuple-element.5, bf16[1,1,128,1024]{3,2,1,0:T(8,128)(2,1)S(1)} %get-tuple-element.2), kind=kLoop, calls=%fused_computation.21 | loop fusion | flops 1572864 | bytes 2097152 | tf_op jit(solution)/shard_map/stack | solution.py:59
  10.5 16.8 %all-to-all-done = bf16[4,96,1024]{2,1,0:T(8,128)(2,1)S(1)} async-done(((bf16[4,96,1024]{2,1,0:T(8,128)(2,1)}), bf16[4,96,1024]{2,1,0:T(8,128)(2,1)S(1)}, u32[]{:S(2)}, u32[]{:S(2)}) %all-to-all-start) | async-done | bytes 786464 | tf_op jit(solution)/shard_map/all_to_all | solution.py:62
  27.3 3.5 %all-to-all-start.1 = ((bf16[4,1,128,1024]{3,2,1,0:T(8,128)(2,1)}), bf16[4,1,128,1024]{3,2,1,0:T(8,128)(2,1)S(1)}, u32[]{:S(2)}, u32[]{:S(2)}) async-start(bf16[4,1,128,1024]{3,2,1,0:T(8,128)(2,1)} %pad_maximum_fusion), calls=%async_computation.1 | async-start | bytes 2097152 | tf_op jit(solution)/shard_map/all_to_all | solution.py:59
  30.8 1.0 %fusion = f32[]{:T(128)} fusion(bf16[4,96,1024]{2,1,0:T(8,128)(2,1)S(1)} %all-to-all-done), kind=kLoop, calls=%fused_computation.2 | loop fusion | flops 1179647 | bytes 786436 | tf_op jit(solution)/shard_map/reduce_sum | solution.py:21
  32.5 0.2 fusion.1
  32.7 0.6 convolution_convert_fusion.2
  33.3 0.8 %add_convert_fusion.1 = bf16[384,1024]{1,0:T(8,128)(2,1)S(1)} fusion(bf16[384,1024]{1,0:T(8,128)(2,1)S(1)} %bitcast.52, bf16[384,384]{1,0:T(8,128)(2,1)S(1)} %convolution_convert_fusion.2), kind=kOutput, calls=%fused_computation.8 | convolution fusion | flops 417546240 | bytes 1867776 | tf_op jit(solution)/shard_map/dot_general | solution.py:32
  34.1 0.9 %copy-done.3 = bf16[384,1024]{1,0:T(8,128)(2,1)} copy-done((bf16[384,1024]{1,0:T(8,128)(2,1)}, bf16[384,1024]{1,0:T(8,128)(2,1)S(1)}, u32[]{:S(2)}) %copy-start.3) | copy-done | bytes 786456
  35.0 0.6 convolution_convert_fusion.1
  35.6 0.5 copy-done.2
  36.1 2.4 %fusion.2 = bf16[384,1024]{1,0:T(8,128)(2,1)S(1)} fusion(bf16[384,1024]{1,0:T(8,128)(2,1)} %copy-done.3, bf16[384,384]{1,0:T(8,128)(2,1)S(1)} %convolution_convert_fusion.1, bf16[1,1,384,1024]{3,2,1,0:T(8,128)(2,1)S(1)} %copy-done.2), kind=kOutput, calls=%fused_computation.5 | convolution fusion | flops 419512320 | bytes 2654208 | tf_op jit(solution)/shard_map/dot_general | solution.py:32
  38.5 1.6 %collective-permute-start = (bf16[384,1024]{1,0:T(8,128)(2,1)S(1)}, bf16[384,1024]{1,0:T(8,128)(2,1)S(1)}, u32[]{:S(2)}, u32[]{:S(2)}) collective-permute-start(bf16[384,1024]{1,0:T(8,128)(2,1)S(1)} %fusion.2), channel_id=1, source_target_pairs={{0,16},{4,20},{8,24},{12,28},{16,0},{20,4},{24,8},{28,12},{1,17},{... | collective-permute-start | bytes 2359304 | tf_op jit(solution)/shard_map/ppermute | solution.py:16
  40.1 17.0 %collective-permute-done = bf16[384,1024]{1,0:T(8,128)(2,1)S(1)} collective-permute-done((bf16[384,1024]{1,0:T(8,128)(2,1)S(1)}, bf16[384,1024]{1,0:T(8,128)(2,1)S(1)}, u32[]{:S(2)}, u32[]{:S(2)}) %collective-permute-start) | collective-permute-done | bytes 786464 | tf_op jit(solution)/shard_map/ppermute | solution.py:16
  57.1 1.2 %fusion.19 = bf16[1,1,384,1024]{3,2,1,0:T(8,128)(2,1)} fusion(bf16[384,1024]{1,0:T(8,128)(2,1)S(1)} %collective-permute-done, bf16[384,1024]{1,0:T(8,128)(2,1)S(1)} %fusion.2), kind=kLoop, calls=%fused_computation.37 | loop fusion | flops 1966080 | bytes 2359296 | tf_op jit(solution)/shard_map/broadcast_in_dim | solution.py:72
  58.3 1.5 %fusion.8 = bf16[1,1,512,384]{3,2,1,0:T(8,128)(2,1)} fusion(bf16[512,1024]{1,0:T(8,128)(2,1)S(1)} %bitcast.49, bf16[384,1024]{1,0:T(8,128)(2,1)S(1)} %collective-permute-done, bf16[384,1024]{1,0:T(8,128)(2,1)S(1)} %fusion.2), kind=kOutput, calls=%fused_computation.20 | convolution fusion | flops 405012480 | bytes 3014656 | tf_op jit(solution)/shard_map/sd,fd->sf/dot_general | solution.py:70
  (11 shorter events, 0.1 us)
Async XLA Ops:
  0.6 8.2 %copy-start = (bf16[1,256,1024]{2,1,0:T(8,128)(2,1)S(1)}, bf16[1,256,1024]{2,1,0:T(8,128)(2,1)}, u32[]{:S(2)}) copy-start(bf16[1,256,1024]{2,1,0:T(8,128)(2,1)} %param.6) | copy-start | bytes 1572868
  0.6 6.5 %copy-start.1 = (s32[1,256,1]{1,2,0:T(1,128)S(1)}, s32[1,256,1]{1,2,0:T(1,128)}, u32[]{:S(2)}) copy-start(s32[1,256,1]{1,2,0:T(1,128)} %param.7) | copy-start | bytes 3076
  0.7 26.6 %all-to-all-start = ((bf16[4,96,1024]{2,1,0:T(8,128)(2,1)}), bf16[4,96,1024]{2,1,0:T(8,128)(2,1)S(1)}, u32[]{:S(2)}, u32[]{:S(2)}) async-start(bf16[4,96,1024]{2,1,0:T(8,128)(2,1)} %bitcast.50), calls=%async_computation | async-start | bytes 1572864 | tf_op jit(solution)/shard_map/all_to_all | solution.py:62
  27.3 31.1 %all-to-all-start.1 = ((bf16[4,1,128,1024]{3,2,1,0:T(8,128)(2,1)}), bf16[4,1,128,1024]{3,2,1,0:T(8,128)(2,1)S(1)}, u32[]{:S(2)}, u32[]{:S(2)}) async-start(bf16[4,1,128,1024]{3,2,1,0:T(8,128)(2,1)} %pad_maximum_fusion), calls=%async_computation.1 | async-start | bytes 2097152 | tf_op jit(solution)/shard_map/all_to_all | solution.py:59
  34.1 0.9 %copy-start.3 = (bf16[384,1024]{1,0:T(8,128)(2,1)}, bf16[384,1024]{1,0:T(8,128)(2,1)S(1)}, u32[]{:S(2)}) copy-start(bf16[384,1024]{1,0:T(8,128)(2,1)S(1)} %add_convert_fusion.1) | copy-start | bytes 2359300
  35.0 1.1 %copy-start.2 = (bf16[1,1,384,1024]{3,2,1,0:T(8,128)(2,1)S(1)}, bf16[1,1,384,1024]{3,2,1,0:T(8,128)(2,1)}, u32[]{:S(2)}) copy-start(bf16[1,1,384,1024]{3,2,1,0:T(8,128)(2,1)} %param.5) | copy-start | bytes 2359300
  38.5 18.6 %collective-permute-start = (bf16[384,1024]{1,0:T(8,128)(2,1)S(1)}, bf16[384,1024]{1,0:T(8,128)(2,1)S(1)}, u32[]{:S(2)}, u32[]{:S(2)}) collective-permute-start(bf16[384,1024]{1,0:T(8,128)(2,1)S(1)} %fusion.2), channel_id=1, source_target_pairs={{0,16},{4,20},{8,24},{12,28},{16,0},{20,4},{24,8},{28,12},{1,17},{... | collective-permute-start | bytes 2359304 | tf_op jit(solution)/shard_map/ppermute | solution.py:16
